TPU v7x, 128 devices: a whole 4x4x4 slice. The times are simulated.
128 devices in a mesh: radar: 8 (over x, core), tile: 16 (over y, z).
Axes of the slice: x: 4, y: 4, z: 4, core: 2. Of those that a mesh axis runs over, the one named last changes fastest.
Arguments:
- background: float32 [3, 256, 32, 2048], P(None, 'tile', None, 'radar'), may hold values from -6 to 6
- interp: bfloat16 [32768, 128, 128], P(('radar', 'tile')), may hold values from -0.5 to 0.5
- beam: bfloat16 [32768, 3, 128], P(('radar', 'tile')), may hold values from -1 to 1
- observed: bfloat16 [32768, 128], P(('radar', 'tile')), may hold values from -6 to 6
- cell_block: int32 [32768], P(('radar', 'tile')), may hold values from 0 to 1023
- sweep_count: int32 [128, 128], P(('radar', 'tile')), may hold values from 0 to 2, as said below
Outputs:
- wind_field: float32 [3, 256, 32, 2048], P(None, 'tile', None, 'radar')
- strain: float32 [6, 256, 32, 2048], P(None, 'tile', None, 'radar')
- cost_trace: float32 [2], replicated
Inputs may be any that keep to these rules, and one draw needn't show every extreme that they name: `cell_block`: the cell block, within the owner's 16 x 32 x 256 cells of one component, read by a slot. `sweep_count`: every source device has an owning device to which all 2 of its slots are live.
All inputs are finite; a program needn't handle non-finite values.
Results may differ from a plain program's by a relative error of at most 0.0014.
Values may be sent and summed in bfloat16 or wider, within the bound.
A program may use at most 64 MiB of HBM per device.

v0:
```python
import jax
import jax.numpy as jnp
from jax import lax
from jax.sharding import Mesh
from jax.sharding import PartitionSpec as P

ITERS = 2
RADAR_TILE = ("radar_0", "radar_1", "tile_0", "tile_1")
RADAR = ("radar_0", "radar_1")
TILE = ("tile_0", "tile_1")
BACKGROUND_WEIGHT = 0.5
DIVERGENCE_WEIGHT = 1.0
STEP_LENGTH = 0.3
EPSILON = 1e-06


def padded_2(x, sides, width):
    edges = {}
    for axis, dim in sides:
        size, length = (lax.axis_size(axis), x.shape[dim])
        up = [(i, (i + 1) % size) for i in range(size - 1)]
        last = lax.slice_in_dim(x, length - width, length, axis=dim)
        first = lax.slice_in_dim(x, 0, width, axis=dim)
        edges[dim] = (
            lax.ppermute(last, axis, up),
            lax.ppermute(first, axis, [(b, a) for a, b in up]),
        )
    done = []
    for _, dim in sides:
        low, high = edges[dim]
        around = [(width, width) if d in done else (0, 0) for d in range(x.ndim)]
        x = jnp.concatenate([jnp.pad(low, around), x, jnp.pad(high, around)], axis=dim)
        done.append(dim)
    return x


def split_up(x, dim, length):
    before, after = (x.shape[:dim], x.shape[dim + 1 :])
    return jnp.moveaxis(x.reshape(*before, length, -1, *after), dim, 0)


def laid_out(tiles, dim):
    tiles = jnp.moveaxis(tiles, 0, dim)
    shape = tiles.shape
    return tiles.reshape(*shape[:dim], shape[dim] * shape[dim + 1], *shape[dim + 2 :])


def joined_exchange(x, axis, axes, splits, concats):
    sizes = [lax.axis_size(a) for a in axes]
    tiles = split_up(x, splits[0], sizes[0])
    tiles = jnp.moveaxis(split_up(tiles, splits[1] + 1, sizes[1]), 0, 1)
    inside = tiles.shape[2:]
    tiles = tiles.reshape(-1, *inside)
    tiles = lax.all_to_all(tiles, axis, split_axis=0, concat_axis=0, tiled=True)
    tiles = laid_out(tiles.reshape(*sizes, *inside), concats[0] + 1)
    return laid_out(tiles, concats[1])


def over_axes(x, axes):
    for axis in axes:
        x = lax.psum(x, axis)
    return x


def vertical_diff(values):
    padded = jnp.pad(values, ((0, 0), (1, 1), (0, 0)))
    return 0.5 * (padded[:, 2:, :] - padded[:, :-2, :])


def along_x(values):
    return 0.5 * (values[2:, :, 1:-1] - values[:-2, :, 1:-1])


def along_y(values):
    return 0.5 * (values[1:-1, :, 2:] - values[1:-1, :, :-2])


def along_z(values):
    return vertical_diff(values[1:-1, :, 1:-1])


def observe(cell_rows, weights, beam_rows, looked, alive_mask):
    projected = jnp.einsum("knc,ngc->nkg", cell_rows, weights, preferred_element_type=jnp.float32)
    beam_values = beam_rows.astype(jnp.float32)
    radial = jnp.sum(beam_values * projected, axis=1)
    misfit = alive_mask[:, None] * (radial - looked.astype(jnp.float32))
    adjoint = (beam_values * misfit[:, None, :]).astype(jnp.bfloat16)
    returned = jnp.einsum("nkg,ngc->knc", adjoint, weights, preferred_element_type=jnp.float32)
    return (0.5 * jnp.sum(misfit * misfit), returned)


def spread_faces(wind_field):
    faces = padded_2(wind_field[:2], ((RADAR, 3), (TILE, 1)), 1)
    spread = along_x(faces[0]) + along_y(faces[1]) + vertical_diff(wind_field[2])
    beside_all = padded_2(spread, ((RADAR, 2), (TILE, 0)), 1)
    push = jnp.stack([-along_x(beside_all), -along_y(beside_all), -vertical_diff(spread)])
    return (spread, push)


def shards(background, interp, beam, observed, cell_block, sweep_count):
    radar_count = lax.axis_size(RADAR)
    tile_count = lax.axis_size(TILE)
    devices = radar_count * tile_count
    width_x = background.shape[1]
    levels = background.shape[2]
    width_y = background.shape[3]
    slots = interp.shape[0] // devices
    gate_size = interp.shape[1]
    block_total = width_x * levels * width_y // gate_size
    total_cells = 3 * width_x * levels * width_y * devices
    total_gates = interp.shape[0] * devices * gate_size
    own_index = cell_block.reshape(devices, slots)
    own_alive = (
        jnp.arange(slots, dtype=jnp.int32)[None, :] < sweep_count.reshape(devices)[:, None]
    ).astype(jnp.int32)
    packed = jnp.stack([own_index, own_alive], 1)
    asked = lax.all_to_all(packed, RADAR_TILE, split_axis=0, concat_axis=0, tiled=True)
    asked_index = asked[:, 0, :].reshape(-1)
    local_alive = own_alive.reshape(-1).astype(jnp.float32)
    wind_field = background
    trace = []
    for step_index in range(ITERS):
        flat = wind_field.reshape(3, block_total, gate_size)
        empty = jnp.zeros((3, block_total, gate_size), jnp.float32)
        chosen = flat[:, asked_index, :].astype(jnp.bfloat16)
        arriving = joined_exchange(
            chosen.reshape(3, radar_count, tile_count, slots, gate_size),
            RADAR_TILE,
            (RADAR, TILE),
            (1, 2),
            (1, 2),
        )
        obs_cost, returned = observe(
            arriving.reshape(3, devices * slots, gate_size), interp, beam, observed, local_alive
        )
        landed = joined_exchange(
            returned.reshape(3, radar_count, tile_count, slots, gate_size),
            RADAR_TILE,
            (RADAR, TILE),
            (1, 2),
            (1, 2),
        )
        obs_cost, obs_flat = (
            obs_cost,
            empty.at[:, asked_index, :].add(landed.reshape(3, devices * slots, gate_size)),
        )
        obs_grad = obs_flat.reshape(wind_field.shape)
        spread, push = spread_faces(wind_field)
        offset = wind_field - background
        gradient = obs_grad + BACKGROUND_WEIGHT * offset + DIVERGENCE_WEIGHT * push
        local_cost = (
            obs_cost
            + 0.5 * BACKGROUND_WEIGHT * jnp.sum(offset * offset)
            + 0.5 * DIVERGENCE_WEIGHT * jnp.sum(spread * spread)
        )
        cost_sum, square_sum = (
            over_axes(local_cost, RADAR_TILE),
            over_axes(jnp.sum(gradient * gradient), RADAR_TILE),
        )
        scale = jnp.sqrt(square_sum / total_cells + EPSILON)
        wind_field = wind_field - STEP_LENGTH * gradient / scale
        trace.append(cost_sum / total_gates)
    faces = padded_2(wind_field, ((RADAR, 3), (TILE, 1)), 1)
    east_wind, north_wind, upward_wind = (faces[0], faces[1], faces[2])
    strain = jnp.stack(
        [
            along_x(east_wind),
            along_y(north_wind),
            along_z(upward_wind),
            0.5 * (along_y(east_wind) + along_x(north_wind)),
            0.5 * (along_z(east_wind) + along_x(upward_wind)),
            0.5 * (along_z(north_wind) + along_y(upward_wind)),
        ]
    )
    return (wind_field, strain, jnp.stack(trace))


def solution(mesh):
    torus = Mesh(mesh.devices.reshape(4, 2, 4, 4), ("radar_0", "radar_1", "tile_0", "tile_1"))
    in_specs = (
        P(None, TILE, None, RADAR),
        P(RADAR_TILE, None, None),
        P(RADAR_TILE, None, None),
        P(RADAR_TILE, None),
        P(RADAR_TILE),
        P(RADAR_TILE, None),
    )
    out_specs = (P(None, TILE, None, RADAR), P(None, TILE, None, RADAR), P())
    return jax.shard_map(
        shards, mesh=torus, in_specs=in_specs, out_specs=out_specs, check_vma=False
    )
```

profile of v0, /device:TPU:98, one launch (start us, length us, event | category | flops | bytes accessed | tf_op | source)
XLA Modules:
  0.0 330.2 jit_solution(9535569945727988790)
XLA Ops:
  0.7 2.4 fusion.83
  5.0 3.6 %collective-permute-start.2 = (f32[2,16,32,1]{3,2,1,0:T(8,128)}, f32[2,16,32,1]{3,2,1,0:T(8,128)}, u32[]{:S(2)}, u32[]{:S(2)}) collective-permute-start(f32[2,16,32,1]{3,2,1,0:T(8,128)} %get-tuple-element.44), channel_id=1, source_target_pairs={{16,0},{32,16},{48,32},{64,48},{80,64},{96,80},{112,96},{17,1},{33... | collective-permute-start | bytes 12296 | tf_op jit(solution)/shard_map/ppermute | solution.py:26
  8.7 2.1 collective-permute-start
  10.8 3.7 %collective-permute-start.3 = (f32[2,1,32,256]{3,2,1,0:T(8,128)S(1)}, f32[2,1,32,256]{3,2,1,0:T(8,128)S(1)}, u32[]{:S(2)}, u32[]{:S(2)}) collective-permute-start(f32[2,1,32,256]{3,2,1,0:T(8,128)S(1)} %get-tuple-element.46), channel_id=1, source_target_pairs={{1,0},{2,1},{3,2},{4,3},{5,4},{6,5},{7,6},{8,7},{9,8},{10,9},{11,1... | collective-permute-start | bytes 196616 | tf_op jit(solution)/shard_map/ppermute | solution.py:26
  15.6 9.8 %all-to-all-start = ((s32[128,2,2]{2,1,0:T(2,128)}), s32[128,2,2]{2,1,0:T(2,128)S(1)}, u32[]{:S(2)}, u32[]{:S(2)}) async-start(s32[128,2,2]{2,1,0:T(2,128)} %copy.39), calls=%async_computation | async-start | bytes 262144 | tf_op jit(solution)/shard_map/all_to_all | solution.py:117
  27.6 4.4 %all-to-all-done = s32[128,2,2]{2,1,0:T(2,128)S(1)} async-done(((s32[128,2,2]{2,1,0:T(2,128)}), s32[128,2,2]{2,1,0:T(2,128)S(1)}, u32[]{:S(2)}, u32[]{:S(2)}) %all-to-all-start) | async-done | bytes 2080 | tf_op jit(solution)/shard_map/all_to_all | solution.py:117
  32.3 2.2 gather_fusion
  35.4 7.7 %all-to-all-start.1 = ((bf16[128,3,1,1,2,128]{5,4,3,2,1,0:T(2,128)(2,1)}), bf16[128,3,1,1,2,128]{5,4,3,2,1,0:T(2,128)(2,1)S(1)}, u32[]{:S(2)}, u32[]{:S(2)}) async-start(bf16[128,3,1,1,2,128]{5,4,3,2,1,0:T(2,128)(2,1)} %bitcast.7), calls=%async_computation.1 | async-start | bytes 393216 | tf_op jit(solution)/shard_map/all_to_all | solution.py:54
  46.2 2.5 collective-permute-start.6
  48.7 5.5 %collective-permute-start.7 = (f32[1,32,256]{2,1,0:T(8,128)S(1)}, f32[1,32,256]{2,1,0:T(8,128)S(1)}, u32[]{:S(2)}, u32[]{:S(2)}) collective-permute-start(f32[1,32,256]{2,1,0:T(8,128)S(1)} %get-tuple-element.58), channel_id=1, source_target_pairs={{0,1},{1,2},{2,3},{3,4},{4,5},{5,6},{6,7},{7,8},{8,9},{9,10},{10,1... | collective-permute-start | bytes 98312 | tf_op jit(solution)/shard_map/ppermute | solution.py:25
  54.3 7.9 %fusion = f32[256,128]{1,0:T(8,128)S(1)} fusion(bf16[3,256,128]{2,0,1:T(4,128)(2,1)S(1)} %bitcast.151, bf16[256,128,128]{2,1,0:T(8,128)(2,1)} %param.7, bf16[256,3,128]{2,0,1:T(8,128)(2,1)S(1)} %copy-done.4), kind=kOutput, calls=%fused_computation.24 | convolution fusion | flops 25427968 | bytes 8912896 | tf_op jit(solution)/shard_map/knc,ngc->nkg/dot_general | solution.py:83
  62.9 5.6 %fusion.66 = f32[256,3,128]{2,1,0:T(4,128)S(1)} fusion(bf16[256,128,128]{2,1,0:T(8,128)(2,1)} %param.7, f32[256,128]{1,0:T(8,128)S(1)} %get-tuple-element.20, bf16[256,3,128]{2,0,1:T(8,128)(2,1)S(1)} %copy-done.4), kind=kOutput, calls=%fused_computation.144 | convolution fusion | flops 25460736 | bytes 9109504 | tf_op jit(solution)/shard_map/nkg,ngc->knc/dot_general | solution.py:88
  69.5 9.7 %all-to-all-start.2 = ((f32[128,3,1,1,2,128]{5,4,3,2,1,0:T(2,128)}), f32[128,3,1,1,2,128]{5,4,3,2,1,0:T(2,128)S(1)}, u32[]{:S(2)}, u32[]{:S(2)}) async-start(f32[128,3,1,1,2,128]{5,4,3,2,1,0:T(2,128)} %bitcast.18), calls=%async_computation.2 | async-start | bytes 786432 | tf_op jit(solution)/shard_map/all_to_all | solution.py:54
  79.4 2.1 collective-permute-start.4
  81.4 3.7 %collective-permute-start.5 = (f32[16,32,1]{2,1,0:T(8,128)S(1)}, f32[16,32,1]{2,1,0:T(8,128)S(1)}, u32[]{:S(2)}, u32[]{:S(2)}) collective-permute-start(f32[16,32,1]{2,1,0:T(8,128)S(1)} %get-tuple-element.59), channel_id=1, source_target_pairs={{16,0},{32,16},{48,32},{64,48},{80,64},{96,80},{112,96},{17,1},{33... | collective-permute-start | bytes 6152 | tf_op jit(solution)/shard_map/ppermute | solution.py:26
  90.9 8.3 %scatter_fusion = f32[3,1024,128]{2,0,1:T(4,128)S(1)} fusion(f32[3,1024,128]{2,0,1:T(4,128)S(1)} %broadcast.90.clone, s32[256]{0:T(256)S(1)} %bitcast.159, f32[256,3,128]{2,1,0:T(4,128)S(1)} %bitcast.147), kind=kCustom, calls=%fused_computation.2 | custom fusion | flops 98304 | bytes 1180672 | tf_op jit(solution)/shard_map/scatter-add | solution.py:145
  102.4 3.0 multiply_reduce_fusion.3
  105.4 9.3 %psum.112 = f32[]{:T(128)} all-reduce(f32[]{:T(128)} %multiply_reduce_fusion.3), channel_id=1, replica_groups=mesh['radar_0'=4,'radar_1'=2,'tile_0'=4,'tile_1'=4] {'radar_0'}, use_global_device_ids=true, to_apply=%region_3.4 | all-reduce | flops 1 | bytes 8 | tf_op jit(solution)/shard_map/psum | solution.py:61
  114.6 3.1 psum.113
  117.8 11.3 %psum.114 = f32[]{:T(128)} all-reduce(f32[]{:T(128)} %psum.113), channel_id=1, replica_groups=mesh['radar_0'=4,'radar_1'=2,'tile_0'=4,'tile_1'=4] {'tile_0'}, use_global_device_ids=true, to_apply=%region_5.6 | all-reduce | flops 1 | bytes 8 | tf_op jit(solution)/shard_map/psum | solution.py:61
  129.1 8.1 %psum.115 = f32[]{:T(128)} all-reduce(f32[]{:T(128)} %psum.114), channel_id=1, replica_groups=mesh['radar_0'=4,'radar_1'=2,'tile_0'=4,'tile_1'=4] {'tile_1'}, use_global_device_ids=true, to_apply=%region_6.7 | all-reduce | flops 1 | bytes 8 | tf_op jit(solution)/shard_map/psum | solution.py:61
  137.9 3.2 multiply_reduce_fusion.1
  144.7 2.4 collective-permute-start.9
  147.2 3.6 %collective-permute-start.11 = (f32[2,1,32,256]{3,2,1,0:T(8,128)}, f32[2,1,32,256]{3,2,1,0:T(8,128)}, u32[]{:S(2)}, u32[]{:S(2)}) collective-permute-start(f32[2,1,32,256]{3,2,1,0:T(8,128)} %get-tuple-element.42), channel_id=1, source_target_pairs={{1,0},{2,1},{3,2},{4,3},{5,4},{6,5},{7,6},{8,7},{9,8},{10,9},{11,1... | collective-permute-start | bytes 196616 | tf_op jit(solution)/shard_map/ppermute | solution.py:26
  150.7 4.4 %collective-permute-start.8 = (f32[2,1,32,256]{3,2,1,0:T(8,128)}, f32[2,1,32,256]{3,2,1,0:T(8,128)}, u32[]{:S(2)}, u32[]{:S(2)}) collective-permute-start(f32[2,1,32,256]{3,2,1,0:T(8,128)} %get-tuple-element.41), channel_id=1, source_target_pairs={{0,1},{1,2},{2,3},{3,4},{4,5},{5,6},{6,7},{7,8},{8,9},{9,10},{10,1... | collective-permute-start | bytes 196616 | tf_op jit(solution)/shard_map/ppermute | solution.py:25
  160.2 2.9 gather_fusion.1
  164.9 8.8 %all-to-all-start.3 = ((bf16[128,3,1,1,2,128]{5,4,3,2,1,0:T(2,128)(2,1)}), bf16[128,3,1,1,2,128]{5,4,3,2,1,0:T(2,128)(2,1)S(1)}, u32[]{:S(2)}, u32[]{:S(2)}) async-start(bf16[128,3,1,1,2,128]{5,4,3,2,1,0:T(2,128)(2,1)} %bitcast.157), calls=%async_computation.3 | async-start | bytes 393216 | tf_op jit(solution)/shard_map/all_to_all | solution.py:54
  173.8 2.3 select_maximum_fusion.2
  179.5 2.5 collective-permute-start.14
  182.0 5.7 %collective-permute-start.15 = (f32[1,32,256]{2,1,0:T(8,128)}, f32[1,32,256]{2,1,0:T(8,128)}, u32[]{:S(2)}, u32[]{:S(2)}) collective-permute-start(f32[1,32,256]{2,1,0:T(8,128)} %get-tuple-element.53), channel_id=1, source_target_pairs={{0,1},{1,2},{2,3},{3,4},{4,5},{5,6},{6,7},{7,8},{8,9},{9,10},{10,1... | collective-permute-start | bytes 98312 | tf_op jit(solution)/shard_map/ppermute | solution.py:25
  187.8 7.9 %fusion.1 = f32[256,128]{1,0:T(8,128)S(1)} fusion(bf16[3,256,128]{2,0,1:T(4,128)(2,1)S(1)} %bitcast.152, bf16[256,128,128]{2,1,0:T(8,128)(2,1)} %param.7, bf16[256,3,128]{2,0,1:T(8,128)(2,1)S(1)} %copy-done.4), kind=kOutput, calls=%fused_computation.25 | convolution fusion | flops 25427968 | bytes 8912896 | tf_op jit(solution)/shard_map/knc,ngc->nkg/dot_general | solution.py:83
  196.5 5.6 %fusion.64 = f32[256,3,128]{2,1,0:T(4,128)S(1)} fusion(bf16[256,128,128]{2,1,0:T(8,128)(2,1)} %param.7, f32[256,128]{1,0:T(8,128)S(1)} %get-tuple-element.25, bf16[256,3,128]{2,0,1:T(8,128)(2,1)S(1)} %copy-done.4), kind=kOutput, calls=%fused_computation.143 | convolution fusion | flops 25460736 | bytes 9109504 | tf_op jit(solution)/shard_map/nkg,ngc->knc/dot_general | solution.py:88
  203.1 9.7 %all-to-all-start.4 = ((f32[128,3,1,1,2,128]{5,4,3,2,1,0:T(2,128)}), f32[128,3,1,1,2,128]{5,4,3,2,1,0:T(2,128)S(1)}, u32[]{:S(2)}, u32[]{:S(2)}) async-start(f32[128,3,1,1,2,128]{5,4,3,2,1,0:T(2,128)} %bitcast.149), calls=%async_computation.4 | async-start | bytes 786432 | tf_op jit(solution)/shard_map/all_to_all | solution.py:54
  214.7 2.0 collective-permute-start.12
  216.8 3.5 %collective-permute-start.13 = (f32[16,32,1]{2,1,0:T(8,128)}, f32[16,32,1]{2,1,0:T(8,128)}, u32[]{:S(2)}, u32[]{:S(2)}) collective-permute-start(f32[16,32,1]{2,1,0:T(8,128)} %get-tuple-element.54), channel_id=1, source_target_pairs={{16,0},{32,16},{48,32},{64,48},{80,64},{96,80},{112,96},{17,1},{33... | collective-permute-start | bytes 6152 | tf_op jit(solution)/shard_map/ppermute | solution.py:26
  224.5 4.3 %fusion.50 = (f32[1,16,32,256]{3,2,1,0:T(8,128)}, f32[1,16,32,256]{3,2,1,0:T(8,128)}, f32[1,16,32,256]{3,2,1,0:T(8,128)}) fusion(f32[1,32,256]{2,1,0:T(8,128)} %collective-permute-done.15, f32[16,32,1]{2,1,0:T(8,128)} %collective-permute-done.13, f32[16,32,256]{2,1,0:T(8,128)} %copy-done.5, f32[16,32,1]{2,1,0:T(8,128)} %collective-permute-done.12, ...), kind=kLoop, calls=%fused_computation.106 | loop fusion | flops 3014656 | bytes 2166784 | tf_op jit(solution)/shard_map/stack | solution.py:96
  232.0 27.8 %scatter_fusion.1 = f32[3,1024,128]{2,0,1:T(4,128)} fusion(f32[3,1024,128]{2,0,1:T(4,128)} %broadcast.90, s32[256]{0:T(256)S(1)} %bitcast.160, f32[256,3,128]{2,1,0:T(4,128)} %bitcast.146), kind=kCustom, calls=%fused_computation.3 | custom fusion | flops 98304 | bytes 1180672 | tf_op jit(solution)/shard_map/scatter-add | solution.py:145
  259.7 2.8 copy.52
  262.6 2.7 reshape.195
  265.3 4.2 %multiply_reduce_fusion.2 = (f32[]{:T(128)}, f32[3,16,32,256]{3,2,1,0:T(8,128)}) fusion(f32[1,16,32,256]{3,2,1,0:T(8,128)} %get-tuple-element.51, f32[1,16,32,256]{3,2,1,0:T(8,128)} %get-tuple-element.48, f32[1,16,32,256]{3,2,1,0:T(8,128)} %get-tuple-element.47, f32[3,16,32,256]{3,2,1,0:T(8,128)} %reshape.195, f32[3,16,32,256]{3,2,1,0:T(8,128)S(1)} %get-tuple-element.23, ...), kind=kLoop, calls=%fused_computation.19 | loop fusion | flops 3145727 | bytes 7864324 | tf_op jit(solution)/shard_map/reduce_sum | solution.py:158
  269.4 9.3 %all-reduce.19 = (f32[]{:T(128)}, f32[]{:T(128)}, f32[]{:T(128)}) all-reduce(f32[]{:T(128)} %get-tuple-element.26, f32[]{:T(128)S(6)} %add.149, f32[]{:T(128)S(6)} %add.147), channel_id=1, replica_groups=mesh['radar_0'=4,'radar_1'=2,'tile_0'=4,'tile_1'=4] {'radar_0'}, use_global_device_ids=true, to_apply=%region_10.11 | all-reduce | flops 3 | bytes 24 | tf_op jit(solution)/shard_map/psum | solution.py:61
  278.7 3.1 all-reduce.20
  281.8 11.3 %all-reduce.18 = (f32[]{:T(128)}, f32[]{:T(128)}, f32[]{:T(128)}) all-reduce(f32[]{:T(128)} %get-tuple-element.14, f32[]{:T(128)} %get-tuple-element.15, f32[]{:T(128)} %get-tuple-element.16), channel_id=1, replica_groups=mesh['radar_0'=4,'radar_1'=2,'tile_0'=4,'tile_1'=4] {'tile_0'}, use_global_device_ids=true, to_apply=%region_12.13 | all-reduce | flops 3 | bytes 24 | tf_op jit(solution)/shard_map/psum | solution.py:61
  293.1 8.1 %all-reduce.17 = (f32[]{:T(128)}, f32[]{:T(128)}, f32[]{:T(128)}) all-reduce(f32[]{:T(128)} %get-tuple-element.8, f32[]{:T(128)} %get-tuple-element.9, f32[]{:T(128)} %get-tuple-element.10), channel_id=1, replica_groups=mesh['radar_0'=4,'radar_1'=2,'tile_0'=4,'tile_1'=4] {'tile_1'}, use_global_device_ids=true, to_apply=%region_13.14 | all-reduce | flops 3 | bytes 24 | tf_op jit(solution)/shard_map/psum | solution.py:61
  308.4 3.6 %collective-permute-start.18 = (f32[3,16,32,1]{2,1,3,0:T(8,128)S(1)}, f32[3,16,32,1]{2,1,3,0:T(8,128)}, u32[]{:S(2)}, u32[]{:S(2)}) collective-permute-start(f32[3,16,32,1]{2,1,3,0:T(8,128)S(1)} %copy.54), channel_id=1, source_target_pairs={{16,0},{32,16},{48,32},{64,48},{80,64},{96,80},{112,96},{17,1},{33... | collective-permute-start | bytes 18440 | tf_op jit(solution)/shard_map/ppermute | solution.py:26
  312.0 4.4 %collective-permute-start.16 = (f32[3,1,32,256]{3,2,1,0:T(8,128)S(1)}, f32[3,1,32,256]{3,2,1,0:T(8,128)S(1)}, u32[]{:S(2)}, u32[]{:S(2)}) collective-permute-start(f32[3,1,32,256]{3,2,1,0:T(8,128)S(1)} %get-tuple-element.37), channel_id=1, source_target_pairs={{0,1},{1,2},{2,3},{3,4},{4,5},{5,6},{6,7},{7,8},{8,9},{9,10},{10,1... | collective-permute-start | bytes 294920 | tf_op jit(solution)/shard_map/ppermute | solution.py:25
  316.5 2.2 collective-permute-start.19
  320.7 4.4 %collective-permute-done.19 = f32[3,1,32,256]{3,2,1,0:T(8,128)S(1)} collective-permute-done((f32[3,1,32,256]{3,2,1,0:T(8,128)S(1)}, f32[3,1,32,256]{3,2,1,0:T(8,128)S(1)}, u32[]{:S(2)}, u32[]{:S(2)}) %collective-permute-start.19) | collective-permute-done | bytes 98336 | tf_op jit(solution)/shard_map/ppermute | solution.py:26
  (117 shorter events, 54.0 us)
Async XLA Ops:
  0.6 8.0 %copy-start = (f32[3,16,32,256]{3,2,1,0:T(8,128)S(1)}, f32[3,16,32,256]{3,2,1,0:T(8,128)}, u32[]{:S(2)}) copy-start(f32[3,16,32,256]{3,2,1,0:T(8,128)} %param.6) | copy-start | bytes 4718596
  0.6 13.9 %copy-start.11 = (s32[1,128]{1,0:T(1,128)S(1)}, s32[1,128]{1,0:T(1,128)}, u32[]{:S(2)}) copy-start(s32[1,128]{1,0:T(1,128)} %param.11) | copy-start | bytes 1540
  0.7 14.0 %copy-start.12 = (s32[256]{0:T(256)S(1)}, s32[256]{0:T(256)}, u32[]{:S(2)}) copy-start(s32[256]{0:T(256)} %param.10) | copy-start | bytes 3076
  3.1 40.0 %collective-permute-start.1 = (f32[2,16,32,1]{3,2,1,0:T(8,128)}, f32[2,16,32,1]{3,2,1,0:T(8,128)}, u32[]{:S(2)}, u32[]{:S(2)}) collective-permute-start(f32[2,16,32,1]{3,2,1,0:T(8,128)} %get-tuple-element.43), channel_id=1, source_target_pairs={{0,16},{16,32},{32,48},{48,64},{64,80},{80,96},{96,112},{1,17},{17... | collective-permute-start | bytes 12296 | tf_op jit(solution)/shard_map/ppermute | solution.py:25
  5.0 38.1 %collective-permute-start.2 = (f32[2,16,32,1]{3,2,1,0:T(8,128)}, f32[2,16,32,1]{3,2,1,0:T(8,128)}, u32[]{:S(2)}, u32[]{:S(2)}) collective-permute-start(f32[2,16,32,1]{3,2,1,0:T(8,128)} %get-tuple-element.44), channel_id=1, source_target_pairs={{16,0},{32,16},{48,32},{64,48},{80,64},{96,80},{112,96},{17,1},{33... | collective-permute-start | bytes 12296 | tf_op jit(solution)/shard_map/ppermute | solution.py:26
  8.7 34.4 %collective-permute-start = (f32[2,1,32,256]{3,2,1,0:T(8,128)S(1)}, f32[2,1,32,256]{3,2,1,0:T(8,128)S(1)}, u32[]{:S(2)}, u32[]{:S(2)}) collective-permute-start(f32[2,1,32,256]{3,2,1,0:T(8,128)S(1)} %get-tuple-element.45), channel_id=1, source_target_pairs={{0,1},{1,2},{2,3},{3,4},{4,5},{5,6},{6,7},{7,8},{8,9},{9,10},{10,1... | collective-permute-start | bytes 196616 | tf_op jit(solution)/shard_map/ppermute | solution.py:25
  10.8 32.3 %collective-permute-start.3 = (f32[2,1,32,256]{3,2,1,0:T(8,128)S(1)}, f32[2,1,32,256]{3,2,1,0:T(8,128)S(1)}, u32[]{:S(2)}, u32[]{:S(2)}) collective-permute-start(f32[2,1,32,256]{3,2,1,0:T(8,128)S(1)} %get-tuple-element.46), channel_id=1, source_target_pairs={{1,0},{2,1},{3,2},{4,3},{5,4},{6,5},{7,6},{8,7},{9,8},{10,9},{11,1... | collective-permute-start | bytes 196616 | tf_op jit(solution)/shard_map/ppermute | solution.py:26
  15.6 16.4 %all-to-all-start = ((s32[128,2,2]{2,1,0:T(2,128)}), s32[128,2,2]{2,1,0:T(2,128)S(1)}, u32[]{:S(2)}, u32[]{:S(2)}) async-start(s32[128,2,2]{2,1,0:T(2,128)} %copy.39), calls=%async_computation | async-start | bytes 262144 | tf_op jit(solution)/shard_map/all_to_all | solution.py:117
  25.8 17.3 %slice-start = ((f32[3,16,32,256]{3,2,1,0:T(8,128)}), f32[2,16,32,256]{3,2,1,0:T(8,128)S(1)}, s32[]{:S(2)}) async-start(f32[3,16,32,256]{3,2,1,0:T(8,128)} %param.6), calls=%async_computation.5 | async-start | bytes 2097152 | tf_op jit(solution)/shard_map/slice | solution.py:93
  35.4 18.8 %all-to-all-start.1 = ((bf16[128,3,1,1,2,128]{5,4,3,2,1,0:T(2,128)(2,1)}), bf16[128,3,1,1,2,128]{5,4,3,2,1,0:T(2,128)(2,1)S(1)}, u32[]{:S(2)}, u32[]{:S(2)}) async-start(bf16[128,3,1,1,2,128]{5,4,3,2,1,0:T(2,128)(2,1)} %bitcast.7), calls=%async_computation.1 | async-start | bytes 393216 | tf_op jit(solution)/shard_map/all_to_all | solution.py:54
  45.1 9.2 %copy-start.4 = (bf16[256,3,128]{2,0,1:T(8,128)(2,1)S(1)}, bf16[256,3,128]{2,0,1:T(8,128)(2,1)}, u32[]{:S(2)}) copy-start(bf16[256,3,128]{2,0,1:T(8,128)(2,1)} %param.8) | copy-start | bytes 589828
  46.2 42.6 %collective-permute-start.6 = (f32[1,32,256]{2,1,0:T(8,128)S(1)}, f32[1,32,256]{2,1,0:T(8,128)S(1)}, u32[]{:S(2)}, u32[]{:S(2)}) collective-permute-start(f32[1,32,256]{2,1,0:T(8,128)S(1)} %get-tuple-element.57), channel_id=1, source_target_pairs={{1,0},{2,1},{3,2},{4,3},{5,4},{6,5},{7,6},{8,7},{9,8},{10,9},{11,1... | collective-permute-start | bytes 98312 | tf_op jit(solution)/shard_map/ppermute | solution.py:26
  48.7 40.1 %collective-permute-start.7 = (f32[1,32,256]{2,1,0:T(8,128)S(1)}, f32[1,32,256]{2,1,0:T(8,128)S(1)}, u32[]{:S(2)}, u32[]{:S(2)}) collective-permute-start(f32[1,32,256]{2,1,0:T(8,128)S(1)} %get-tuple-element.58), channel_id=1, source_target_pairs={{0,1},{1,2},{2,3},{3,4},{4,5},{5,6},{6,7},{7,8},{8,9},{9,10},{10,1... | collective-permute-start | bytes 98312 | tf_op jit(solution)/shard_map/ppermute | solution.py:25
  54.3 7.9 %copy-start.8 = (bf16[256,128]{1,0:T(8,128)(2,1)S(1)}, bf16[256,128]{1,0:T(8,128)(2,1)}, u32[]{:S(2)}) copy-start(bf16[256,128]{1,0:T(8,128)(2,1)} %param.9) | copy-start | bytes 196612
  69.5 21.0 %all-to-all-start.2 = ((f32[128,3,1,1,2,128]{5,4,3,2,1,0:T(2,128)}), f32[128,3,1,1,2,128]{5,4,3,2,1,0:T(2,128)S(1)}, u32[]{:S(2)}, u32[]{:S(2)}) async-start(f32[128,3,1,1,2,128]{5,4,3,2,1,0:T(2,128)} %bitcast.18), calls=%async_computation.2 | async-start | bytes 786432 | tf_op jit(solution)/shard_map/all_to_all | solution.py:54
  79.4 7.8 %collective-permute-start.4 = (f32[16,32,1]{2,1,0:T(8,128)S(1)}, f32[16,32,1]{2,1,0:T(8,128)S(1)}, u32[]{:S(2)}, u32[]{:S(2)}) collective-permute-start(f32[16,32,1]{2,1,0:T(8,128)S(1)} %get-tuple-element.60), channel_id=1, source_target_pairs={{0,16},{16,32},{32,48},{48,64},{64,80},{80,96},{96,112},{1,17},{17... | collective-permute-start | bytes 6152 | tf_op jit(solution)/shard_map/ppermute | solution.py:25
  81.4 7.4 %collective-permute-start.5 = (f32[16,32,1]{2,1,0:T(8,128)S(1)}, f32[16,32,1]{2,1,0:T(8,128)S(1)}, u32[]{:S(2)}, u32[]{:S(2)}) collective-permute-start(f32[16,32,1]{2,1,0:T(8,128)S(1)} %get-tuple-element.59), channel_id=1, source_target_pairs={{16,0},{32,16},{48,32},{64,48},{80,64},{96,80},{112,96},{17,1},{33... | collective-permute-start | bytes 6152 | tf_op jit(solution)/shard_map/ppermute | solution.py:26
  100.5 1.9 copy-start.1
  102.3 3.0 copy-start.3
  142.8 30.9 %collective-permute-start.10 = (f32[2,16,32,1]{3,2,1,0:T(8,128)}, f32[2,16,32,1]{3,2,1,0:T(8,128)}, u32[]{:S(2)}, u32[]{:S(2)}) collective-permute-start(f32[2,16,32,1]{3,2,1,0:T(8,128)} %get-tuple-element.40), channel_id=1, source_target_pairs={{16,0},{32,16},{48,32},{64,48},{80,64},{96,80},{112,96},{17,1},{33... | collective-permute-start | bytes 12296 | tf_op jit(solution)/shard_map/ppermute | solution.py:26
  144.7 29.0 %collective-permute-start.9 = (f32[2,16,32,1]{3,2,1,0:T(8,128)}, f32[2,16,32,1]{3,2,1,0:T(8,128)}, u32[]{:S(2)}, u32[]{:S(2)}) collective-permute-start(f32[2,16,32,1]{3,2,1,0:T(8,128)} %get-tuple-element.39), channel_id=1, source_target_pairs={{0,16},{16,32},{32,48},{48,64},{64,80},{80,96},{96,112},{1,17},{17... | collective-permute-start | bytes 12296 | tf_op jit(solution)/shard_map/ppermute | solution.py:25
  147.2 26.6 %collective-permute-start.11 = (f32[2,1,32,256]{3,2,1,0:T(8,128)}, f32[2,1,32,256]{3,2,1,0:T(8,128)}, u32[]{:S(2)}, u32[]{:S(2)}) collective-permute-start(f32[2,1,32,256]{3,2,1,0:T(8,128)} %get-tuple-element.42), channel_id=1, source_target_pairs={{1,0},{2,1},{3,2},{4,3},{5,4},{6,5},{7,6},{8,7},{9,8},{10,9},{11,1... | collective-permute-start | bytes 196616 | tf_op jit(solution)/shard_map/ppermute | solution.py:26
  150.7 23.0 %collective-permute-start.8 = (f32[2,1,32,256]{3,2,1,0:T(8,128)}, f32[2,1,32,256]{3,2,1,0:T(8,128)}, u32[]{:S(2)}, u32[]{:S(2)}) collective-permute-start(f32[2,1,32,256]{3,2,1,0:T(8,128)} %get-tuple-element.41), channel_id=1, source_target_pairs={{0,1},{1,2},{2,3},{3,4},{4,5},{5,6},{6,7},{7,8},{8,9},{9,10},{10,1... | collective-permute-start | bytes 196616 | tf_op jit(solution)/shard_map/ppermute | solution.py:25
  157.0 1.5 copy-start.6
  164.9 22.8 %all-to-all-start.3 = ((bf16[128,3,1,1,2,128]{5,4,3,2,1,0:T(2,128)(2,1)}), bf16[128,3,1,1,2,128]{5,4,3,2,1,0:T(2,128)(2,1)S(1)}, u32[]{:S(2)}, u32[]{:S(2)}) async-start(bf16[128,3,1,1,2,128]{5,4,3,2,1,0:T(2,128)(2,1)} %bitcast.157), calls=%async_computation.3 | async-start | bytes 393216 | tf_op jit(solution)/shard_map/all_to_all | solution.py:54
  176.0 1.0 copy-start.7
  178.1 0.8 copy-start.5
  179.5 45.0 %collective-permute-start.14 = (f32[1,32,256]{2,1,0:T(8,128)}, f32[1,32,256]{2,1,0:T(8,128)}, u32[]{:S(2)}, u32[]{:S(2)}) collective-permute-start(f32[1,32,256]{2,1,0:T(8,128)} %get-tuple-element.52), channel_id=1, source_target_pairs={{1,0},{2,1},{3,2},{4,3},{5,4},{6,5},{7,6},{8,7},{9,8},{10,9},{11,1... | collective-permute-start | bytes 98312 | tf_op jit(solution)/shard_map/ppermute | solution.py:26
  182.0 42.5 %collective-permute-start.15 = (f32[1,32,256]{2,1,0:T(8,128)}, f32[1,32,256]{2,1,0:T(8,128)}, u32[]{:S(2)}, u32[]{:S(2)}) collective-permute-start(f32[1,32,256]{2,1,0:T(8,128)} %get-tuple-element.53), channel_id=1, source_target_pairs={{0,1},{1,2},{2,3},{3,4},{4,5},{5,6},{6,7},{7,8},{8,9},{9,10},{10,1... | collective-permute-start | bytes 98312 | tf_op jit(solution)/shard_map/ppermute | solution.py:25
  187.8 7.9 %copy-start.9 = (bf16[256,128]{1,0:T(8,128)(2,1)S(1)}, bf16[256,128]{1,0:T(8,128)(2,1)}, u32[]{:S(2)}) copy-start(bf16[256,128]{1,0:T(8,128)(2,1)} %param.9) | copy-start | bytes 196612
  203.1 26.4 %all-to-all-start.4 = ((f32[128,3,1,1,2,128]{5,4,3,2,1,0:T(2,128)}), f32[128,3,1,1,2,128]{5,4,3,2,1,0:T(2,128)S(1)}, u32[]{:S(2)}, u32[]{:S(2)}) async-start(f32[128,3,1,1,2,128]{5,4,3,2,1,0:T(2,128)} %bitcast.149), calls=%async_computation.4 | async-start | bytes 786432 | tf_op jit(solution)/shard_map/all_to_all | solution.py:54
  214.7 8.6 %collective-permute-start.12 = (f32[16,32,1]{2,1,0:T(8,128)}, f32[16,32,1]{2,1,0:T(8,128)}, u32[]{:S(2)}, u32[]{:S(2)}) collective-permute-start(f32[16,32,1]{2,1,0:T(8,128)} %get-tuple-element.55), channel_id=1, source_target_pairs={{0,16},{16,32},{32,48},{48,64},{64,80},{80,96},{96,112},{1,17},{17... | collective-permute-start | bytes 6152 | tf_op jit(solution)/shard_map/ppermute | solution.py:25
  216.8 7.7 %collective-permute-start.13 = (f32[16,32,1]{2,1,0:T(8,128)}, f32[16,32,1]{2,1,0:T(8,128)}, u32[]{:S(2)}, u32[]{:S(2)}) collective-permute-start(f32[16,32,1]{2,1,0:T(8,128)} %get-tuple-element.54), channel_id=1, source_target_pairs={{16,0},{32,16},{48,32},{64,48},{80,64},{96,80},{112,96},{17,1},{33... | collective-permute-start | bytes 6152 | tf_op jit(solution)/shard_map/ppermute | solution.py:26
  303.6 21.5 %copy-start.2 = (f32[3,16,32,256]{3,2,1,0:T(8,128)}, f32[3,16,32,256]{3,2,1,0:T(8,128)S(1)}, u32[]{:S(2)}) copy-start(f32[3,16,32,256]{3,2,1,0:T(8,128)S(1)} %divide_subtract_fusion) | copy-start | bytes 4718596
  306.1 13.1 %collective-permute-start.17 = (f32[3,16,32,1]{2,1,3,0:T(8,128)}, f32[3,16,32,1]{2,1,3,0:T(8,128)S(1)}, u32[]{:S(2)}, u32[]{:S(2)}) collective-permute-start(f32[3,16,32,1]{2,1,3,0:T(8,128)} %copy.53), channel_id=1, source_target_pairs={{0,16},{16,32},{32,48},{48,64},{64,80},{80,96},{96,112},{1,17},{17... | collective-permute-start | bytes 18440 | tf_op jit(solution)/shard_map/ppermute | solution.py:25
  308.4 11.2 %collective-permute-start.18 = (f32[3,16,32,1]{2,1,3,0:T(8,128)S(1)}, f32[3,16,32,1]{2,1,3,0:T(8,128)}, u32[]{:S(2)}, u32[]{:S(2)}) collective-permute-start(f32[3,16,32,1]{2,1,3,0:T(8,128)S(1)} %copy.54), channel_id=1, source_target_pairs={{16,0},{32,16},{48,32},{64,48},{80,64},{96,80},{112,96},{17,1},{33... | collective-permute-start | bytes 18440 | tf_op jit(solution)/shard_map/ppermute | solution.py:26
  312.0 8.7 %collective-permute-start.16 = (f32[3,1,32,256]{3,2,1,0:T(8,128)S(1)}, f32[3,1,32,256]{3,2,1,0:T(8,128)S(1)}, u32[]{:S(2)}, u32[]{:S(2)}) collective-permute-start(f32[3,1,32,256]{3,2,1,0:T(8,128)S(1)} %get-tuple-element.37), channel_id=1, source_target_pairs={{0,1},{1,2},{2,3},{3,4},{4,5},{5,6},{6,7},{7,8},{8,9},{9,10},{10,1... | collective-permute-start | bytes 294920 | tf_op jit(solution)/shard_map/ppermute | solution.py:25
  316.5 8.6 %collective-permute-start.19 = (f32[3,1,32,256]{3,2,1,0:T(8,128)S(1)}, f32[3,1,32,256]{3,2,1,0:T(8,128)S(1)}, u32[]{:S(2)}, u32[]{:S(2)}) collective-permute-start(f32[3,1,32,256]{3,2,1,0:T(8,128)S(1)} %get-tuple-element.38), channel_id=1, source_target_pairs={{1,0},{2,1},{3,2},{4,3},{5,4},{6,5},{7,6},{8,7},{9,8},{10,9},{11,1... | collective-permute-start | bytes 294920 | tf_op jit(solution)/shard_map/ppermute | solution.py:26
  328.6 1.7 copy-start.10
where the time goes:
time: 333 us; the launch traced here: 330 us
  starting transfers between devices  109 us (33%)
  other arithmetic  65.3 us (20%)
  blocking collectives  63.6 us (19%)
  local copies, waits for them, and re-layouts  44.1 us (13%)
  matrix products  27 us (8%)
  waiting for transfers between devices  13.7 us (4%)
  between operations  7.62 us (2%)
    psum x8, blocking collectives, over_axes(): x = lax.psum(x, axis)  63.6 us
    scatter-add x2, other arithmetic, shards(): empty.at[:, asked_index, :]  36.1 us
    all_to_all x4, starting transfers between devices, joined_exchange(): tiles = lax.all_to_all(tiles, axis, split_axis=0, concat_axis=0, tiled=True)  36 us
    ppermute x10, starting transfers between devices, padded_2(): lax.ppermute(last, axis, up)  32.4 us
    ppermute x10, starting transfers between devices, padded_2(): lax.ppermute(first, axis, [(b, a) for a, b in up])  30.8 us
    dot_general x2, matrix products, observe(): jnp.einsum('knc,ngc->nkg', cell_rows, weights, preferred_element_type=jnp...  15.7 us
    dot_general x2, matrix products, observe(): jnp.einsum('nkg,ngc->knc', adjoint, weights, preferred_element_type=jnp.f...  11.3 us
    all_to_all x1, starting transfers between devices, shards(): lax.all_to_all(packed, RADAR_TILE, split_axis=0, concat_axis=0, tiled=True)  9.84 us
  transfers between devices with their start and end apart: 25, of which 5 were waited for; matrix products, arithmetic and copies ran while one was open for 19% of the time, Pallas kernels for 0%

commit v1 on v0

--- a/solution.py
+++ b/solution.py
@@ -58,7 +58,7 @@
 
 def over_axes(x, axes):
     for axis in axes:
-        x = lax.psum(x, axis)
+        x = jnp.sum(lax.all_gather(x, axis), axis=0)
     return x
 
 

time: 333 us -> 360 us (1.081)
  local copies, waits for them, and re-layouts: 44.1 us -> 67 us
  other arithmetic: 65.3 us -> 75.3 us
  blocking collectives: 63.6 us -> 58.1 us
    psum x8 -> x0, blocking collectives: 63.6 us -> none  [over_axes(): x = lax.psum(x, axis)]
    unnamed x0 -> x8, blocking collectives: none -> 58.1 us
    unnamed x26 -> x70, local copies, waits for them, and re-layouts: 3.87 us -> 26.8 us
    reduce_sum x0 -> x16, other arithmetic: none -> 9.96 us  [over_axes(): x = jnp.sum(lax.all_gather(x, axis), axis=0)]
  transfers between devices with their start and end apart: 25 -> 25, of which waited for: 5 -> 5; matrix products, arithmetic and copies ran while one was open for 19% -> 18% of each run, Pallas kernels for 0% -> 0%
where the time goes in v1:
time: 360 us; the launch traced here: 357 us
  starting transfers between devices  109 us (30%)
  other arithmetic  75.3 us (21%)
  local copies, waits for them, and re-layouts  67 us (19%)
  blocking collectives  58.1 us (16%)
  matrix products  27 us (8%)
  waiting for transfers between devices  12.3 us (3%)
  between operations  7.93 us (2%)
    unnamed x8, blocking collectives  58.1 us
    scatter-add x2, other arithmetic, shards(): empty.at[:, asked_index, :]  36.1 us
    all_to_all x4, starting transfers between devices, joined_exchange(): tiles = lax.all_to_all(tiles, axis, split_axis=0, concat_axis=0, tiled=True)  36 us
    ppermute x10, starting transfers between devices, padded_2(): lax.ppermute(last, axis, up)  32.4 us
    ppermute x10, starting transfers between devices, padded_2(): lax.ppermute(first, axis, [(b, a) for a, b in up])  30.8 us
    unnamed x70, local copies, waits for them, and re-layouts  26.8 us
    dot_general x2, matrix products, observe(): jnp.einsum('knc,ngc->nkg', cell_rows, weights, preferred_element_type=jnp...  15.7 us
    dot_general x2, matrix products, observe(): jnp.einsum('nkg,ngc->knc', adjoint, weights, preferred_element_type=jnp.f...  11.3 us
  transfers between devices with their start and end apart: 25, of which 5 were waited for; matrix products, arithmetic and copies ran while one was open for 18% of the time, Pallas kernels for 0%

profile of v1, /device:TPU:98, one launch (start us, length us, event | category | flops | bytes accessed | tf_op | source)
XLA Modules:
  0.0 356.6 jit_solution(417610631183465954)
XLA Ops:
  0.7 2.4 fusion.83
  5.0 3.6 %collective-permute-start.2 = (f32[2,16,32,1]{3,2,1,0:T(8,128)}, f32[2,16,32,1]{3,2,1,0:T(8,128)}, u32[]{:S(2)}, u32[]{:S(2)}) collective-permute-start(f32[2,16,32,1]{3,2,1,0:T(8,128)} %get-tuple-element.44), channel_id=1, source_target_pairs={{16,0},{32,16},{48,32},{64,48},{80,64},{96,80},{112,96},{17,1},{33... | collective-permute-start | bytes 12296 | tf_op jit(solution)/shard_map/ppermute | solution.py:26
  8.7 2.1 collective-permute-start
  10.8 3.7 %collective-permute-start.3 = (f32[2,1,32,256]{3,2,1,0:T(8,128)S(1)}, f32[2,1,32,256]{3,2,1,0:T(8,128)S(1)}, u32[]{:S(2)}, u32[]{:S(2)}) collective-permute-start(f32[2,1,32,256]{3,2,1,0:T(8,128)S(1)} %get-tuple-element.46), channel_id=1, source_target_pairs={{1,0},{2,1},{3,2},{4,3},{5,4},{6,5},{7,6},{8,7},{9,8},{10,9},{11,1... | collective-permute-start | bytes 196616 | tf_op jit(solution)/shard_map/ppermute | solution.py:26
  15.6 9.8 %all-to-all-start = ((s32[128,2,2]{2,1,0:T(2,128)}), s32[128,2,2]{2,1,0:T(2,128)S(1)}, u32[]{:S(2)}, u32[]{:S(2)}) async-start(s32[128,2,2]{2,1,0:T(2,128)} %copy.39), calls=%async_computation | async-start | bytes 262144 | tf_op jit(solution)/shard_map/all_to_all | solution.py:117
  27.6 4.4 %all-to-all-done = s32[128,2,2]{2,1,0:T(2,128)S(1)} async-done(((s32[128,2,2]{2,1,0:T(2,128)}), s32[128,2,2]{2,1,0:T(2,128)S(1)}, u32[]{:S(2)}, u32[]{:S(2)}) %all-to-all-start) | async-done | bytes 2080 | tf_op jit(solution)/shard_map/all_to_all | solution.py:117
  32.3 2.2 gather_fusion
  35.4 7.7 %all-to-all-start.1 = ((bf16[128,3,1,1,2,128]{5,4,3,2,1,0:T(2,128)(2,1)}), bf16[128,3,1,1,2,128]{5,4,3,2,1,0:T(2,128)(2,1)S(1)}, u32[]{:S(2)}, u32[]{:S(2)}) async-start(bf16[128,3,1,1,2,128]{5,4,3,2,1,0:T(2,128)(2,1)} %bitcast.7), calls=%async_computation.1 | async-start | bytes 393216 | tf_op jit(solution)/shard_map/all_to_all | solution.py:54
  46.2 2.5 collective-permute-start.6
  48.7 5.5 %collective-permute-start.7 = (f32[1,32,256]{2,1,0:T(8,128)S(1)}, f32[1,32,256]{2,1,0:T(8,128)S(1)}, u32[]{:S(2)}, u32[]{:S(2)}) collective-permute-start(f32[1,32,256]{2,1,0:T(8,128)S(1)} %get-tuple-element.58), channel_id=1, source_target_pairs={{0,1},{1,2},{2,3},{3,4},{4,5},{5,6},{6,7},{7,8},{8,9},{9,10},{10,1... | collective-permute-start | bytes 98312 | tf_op jit(solution)/shard_map/ppermute | solution.py:25
  54.3 7.9 %fusion = f32[256,128]{1,0:T(8,128)S(1)} fusion(bf16[3,256,128]{2,0,1:T(4,128)(2,1)S(1)} %bitcast.171, bf16[256,128,128]{2,1,0:T(8,128)(2,1)} %param.7, bf16[256,3,128]{2,0,1:T(8,128)(2,1)S(1)} %copy-done.4), kind=kOutput, calls=%fused_computation.24 | convolution fusion | flops 25427968 | bytes 8912896 | tf_op jit(solution)/shard_map/knc,ngc->nkg/dot_general | solution.py:83
  62.8 5.6 %fusion.66 = f32[256,3,128]{2,1,0:T(4,128)S(1)} fusion(bf16[256,128,128]{2,1,0:T(8,128)(2,1)} %param.7, f32[256,128]{1,0:T(8,128)S(1)} %get-tuple-element.20, bf16[256,3,128]{2,0,1:T(8,128)(2,1)S(1)} %copy-done.4), kind=kOutput, calls=%fused_computation.144 | convolution fusion | flops 25460736 | bytes 9109504 | tf_op jit(solution)/shard_map/nkg,ngc->knc/dot_general | solution.py:88
  69.4 9.7 %all-to-all-start.2 = ((f32[128,3,1,1,2,128]{5,4,3,2,1,0:T(2,128)}), f32[128,3,1,1,2,128]{5,4,3,2,1,0:T(2,128)S(1)}, u32[]{:S(2)}, u32[]{:S(2)}) async-start(f32[128,3,1,1,2,128]{5,4,3,2,1,0:T(2,128)} %bitcast.18), calls=%async_computation.2 | async-start | bytes 786432 | tf_op jit(solution)/shard_map/all_to_all | solution.py:54
  79.3 2.1 collective-permute-start.4
  81.4 3.7 %collective-permute-start.5 = (f32[16,32,1]{2,1,0:T(8,128)S(1)}, f32[16,32,1]{2,1,0:T(8,128)S(1)}, u32[]{:S(2)}, u32[]{:S(2)}) collective-permute-start(f32[16,32,1]{2,1,0:T(8,128)S(1)} %get-tuple-element.59), channel_id=1, source_target_pairs={{16,0},{32,16},{48,32},{64,48},{80,64},{96,80},{112,96},{17,1},{33... | collective-permute-start | bytes 6152 | tf_op jit(solution)/shard_map/ppermute | solution.py:26
  90.9 8.3 %scatter_fusion = f32[3,1024,128]{2,0,1:T(4,128)S(1)} fusion(f32[3,1024,128]{2,0,1:T(4,128)S(1)} %broadcast.90.clone, s32[256]{0:T(256)S(1)} %bitcast.179, f32[256,3,128]{2,1,0:T(4,128)S(1)} %bitcast.167), kind=kCustom, calls=%fused_computation.2 | custom fusion | flops 98304 | bytes 1180672 | tf_op jit(solution)/shard_map/scatter-add | solution.py:145
  102.4 3.0 multiply_reduce_fusion.3
  107.2 8.6 %all-reduce.17 = f32[4]{0:T(128)S(1)} all-reduce(f32[4]{0:T(128)S(1)} %dynamic-update-slice), channel_id=1, replica_groups=mesh['radar_0'=4,'radar_1'=2,'tile_0'=4,'tile_1'=4] {'radar_0'}, use_global_device_ids=true, to_apply=%add.17 | all-reduce | flops 4 | bytes 32
  118.6 2.4 all-reduce.18
  123.6 10.6 %all-reduce.19 = f32[4]{0:T(128)S(1)} all-reduce(f32[4]{0:T(128)S(1)} %dynamic-update-slice.2), channel_id=1, replica_groups=mesh['radar_0'=4,'radar_1'=2,'tile_0'=4,'tile_1'=4] {'tile_0'}, use_global_device_ids=true, to_apply=%add.19 | all-reduce | flops 4 | bytes 32
  136.2 7.4 %all-reduce.20 = f32[4]{0:T(128)S(1)} all-reduce(f32[4]{0:T(128)S(1)} %dynamic-update-slice.3), channel_id=1, replica_groups=mesh['radar_0'=4,'radar_1'=2,'tile_0'=4,'tile_1'=4] {'tile_1'}, use_global_device_ids=true, to_apply=%add.20 | all-reduce | flops 4 | bytes 32
  145.1 3.2 multiply_reduce_fusion.1
  152.0 2.4 collective-permute-start.9
  154.4 3.6 %collective-permute-start.11 = (f32[2,1,32,256]{3,2,1,0:T(8,128)}, f32[2,1,32,256]{3,2,1,0:T(8,128)}, u32[]{:S(2)}, u32[]{:S(2)}) collective-permute-start(f32[2,1,32,256]{3,2,1,0:T(8,128)} %get-tuple-element.42), channel_id=1, source_target_pairs={{1,0},{2,1},{3,2},{4,3},{5,4},{6,5},{7,6},{8,7},{9,8},{10,9},{11,1... | collective-permute-start | bytes 196616 | tf_op jit(solution)/shard_map/ppermute | solution.py:26
  158.0 4.4 %collective-permute-start.8 = (f32[2,1,32,256]{3,2,1,0:T(8,128)}, f32[2,1,32,256]{3,2,1,0:T(8,128)}, u32[]{:S(2)}, u32[]{:S(2)}) collective-permute-start(f32[2,1,32,256]{3,2,1,0:T(8,128)} %get-tuple-element.41), channel_id=1, source_target_pairs={{0,1},{1,2},{2,3},{3,4},{4,5},{5,6},{6,7},{7,8},{8,9},{9,10},{10,1... | collective-permute-start | bytes 196616 | tf_op jit(solution)/shard_map/ppermute | solution.py:25
  167.4 2.9 gather_fusion.1
  172.1 8.8 %all-to-all-start.3 = ((bf16[128,3,1,1,2,128]{5,4,3,2,1,0:T(2,128)(2,1)}), bf16[128,3,1,1,2,128]{5,4,3,2,1,0:T(2,128)(2,1)S(1)}, u32[]{:S(2)}, u32[]{:S(2)}) async-start(bf16[128,3,1,1,2,128]{5,4,3,2,1,0:T(2,128)(2,1)} %bitcast.177), calls=%async_computation.3 | async-start | bytes 393216 | tf_op jit(solution)/shard_map/all_to_all | solution.py:54
  181.0 2.3 select_maximum_fusion.2
  186.8 2.5 collective-permute-start.14
  189.3 5.7 %collective-permute-start.15 = (f32[1,32,256]{2,1,0:T(8,128)}, f32[1,32,256]{2,1,0:T(8,128)}, u32[]{:S(2)}, u32[]{:S(2)}) collective-permute-start(f32[1,32,256]{2,1,0:T(8,128)} %get-tuple-element.53), channel_id=1, source_target_pairs={{0,1},{1,2},{2,3},{3,4},{4,5},{5,6},{6,7},{7,8},{8,9},{9,10},{10,1... | collective-permute-start | bytes 98312 | tf_op jit(solution)/shard_map/ppermute | solution.py:25
  195.1 7.9 %fusion.1 = f32[256,128]{1,0:T(8,128)S(1)} fusion(bf16[3,256,128]{2,0,1:T(4,128)(2,1)S(1)} %bitcast.172, bf16[256,128,128]{2,1,0:T(8,128)(2,1)} %param.7, bf16[256,3,128]{2,0,1:T(8,128)(2,1)S(1)} %copy-done.4), kind=kOutput, calls=%fused_computation.25 | convolution fusion | flops 25427968 | bytes 8912896 | tf_op jit(solution)/shard_map/knc,ngc->nkg/dot_general | solution.py:83
  203.8 5.6 %fusion.64 = f32[256,3,128]{2,1,0:T(4,128)S(1)} fusion(bf16[256,128,128]{2,1,0:T(8,128)(2,1)} %param.7, f32[256,128]{1,0:T(8,128)S(1)} %get-tuple-element.25, bf16[256,3,128]{2,0,1:T(8,128)(2,1)S(1)} %copy-done.4), kind=kOutput, calls=%fused_computation.143 | convolution fusion | flops 25460736 | bytes 9109504 | tf_op jit(solution)/shard_map/nkg,ngc->knc/dot_general | solution.py:88
  210.4 9.7 %all-to-all-start.4 = ((f32[128,3,1,1,2,128]{5,4,3,2,1,0:T(2,128)}), f32[128,3,1,1,2,128]{5,4,3,2,1,0:T(2,128)S(1)}, u32[]{:S(2)}, u32[]{:S(2)}) async-start(f32[128,3,1,1,2,128]{5,4,3,2,1,0:T(2,128)} %bitcast.169), calls=%async_computation.4 | async-start | bytes 786432 | tf_op jit(solution)/shard_map/all_to_all | solution.py:54
  222.0 2.0 collective-permute-start.12
  224.1 3.5 collective-permute-start.13
  231.8 4.4 %fusion.50 = (f32[1,16,32,256]{3,2,1,0:T(8,128)}, f32[1,16,32,256]{3,2,1,0:T(8,128)}, f32[1,16,32,256]{3,2,1,0:T(8,128)}) fusion(f32[1,32,256]{2,1,0:T(8,128)} %collective-permute-done.15, f32[16,32,1]{2,1,0:T(8,128)} %collective-permute-done.13, f32[16,32,256]{2,1,0:T(8,128)} %copy-done.5, f32[16,32,1]{2,1,0:T(8,128)} %collective-permute-done.12, ...), kind=kLoop, calls=%fused_computation.106 | loop fusion | flops 3014656 | bytes 2166784 | tf_op jit(solution)/shard_map/stack | solution.py:96
  240.0 27.8 %scatter_fusion.1 = f32[3,1024,128]{2,0,1:T(4,128)} fusion(f32[3,1024,128]{2,0,1:T(4,128)} %broadcast.90, s32[256]{0:T(256)S(1)} %bitcast.180, f32[256,3,128]{2,1,0:T(4,128)} %bitcast.166), kind=kCustom, calls=%fused_computation.3 | custom fusion | flops 98304 | bytes 1180672 | tf_op jit(solution)/shard_map/scatter-add | solution.py:145
  267.7 2.8 copy.52
  270.6 2.7 reshape.195
  273.2 4.2 %multiply_reduce_fusion.2 = (f32[]{:T(128)}, f32[3,16,32,256]{3,2,1,0:T(8,128)}) fusion(f32[1,16,32,256]{3,2,1,0:T(8,128)} %get-tuple-element.51, f32[1,16,32,256]{3,2,1,0:T(8,128)} %get-tuple-element.48, f32[1,16,32,256]{3,2,1,0:T(8,128)} %get-tuple-element.47, f32[3,16,32,256]{3,2,1,0:T(8,128)} %reshape.195, f32[3,16,32,256]{3,2,1,0:T(8,128)S(1)} %get-tuple-element.23, ...), kind=kLoop, calls=%fused_computation.19 | loop fusion | flops 3145727 | bytes 7864324 | tf_op jit(solution)/shard_map/reduce_sum | solution.py:158
  278.7 8.6 %all-reduce.35 = (f32[4]{0:T(128)S(1)}, f32[4]{0:T(128)S(1)}, f32[4]{0:T(128)S(1)}) all-reduce(f32[4]{0:T(128)S(1)} %dynamic-update-slice.4, f32[4]{0:T(128)S(1)} %dynamic-update-slice.12, f32[4]{0:T(128)S(1)} %dynamic-update-slice.8), channel_id=1, replica_groups=mesh['radar_0'=4,'radar_1'=2,'tile_0'=4,'tile_1'=4] {'radar_0'}, use_global_device_ids=true, to_apply=%add.21 | all-reduce | flops 12 | bytes 96
  293.2 2.4 all-reduce.36
  301.8 10.6 %all-reduce.34 = (f32[4]{0:T(128)S(1)}, f32[4]{0:T(128)S(1)}, f32[4]{0:T(128)S(1)}) all-reduce(f32[4]{0:T(128)S(1)} %dynamic-update-slice.6, f32[4]{0:T(128)S(1)} %dynamic-update-slice.14, f32[4]{0:T(128)S(1)} %dynamic-update-slice.10), channel_id=1, replica_groups=mesh['radar_0'=4,'radar_1'=2,'tile_0'=4,'tile_1'=4] {'tile_0'}, use_global_device_ids=true, to_apply=%add.23 | all-reduce | flops 12 | bytes 96
  318.2 7.4 %all-reduce.33 = (f32[4]{0:T(128)S(1)}, f32[4]{0:T(128)S(1)}, f32[4]{0:T(128)S(1)}) all-reduce(f32[4]{0:T(128)S(1)} %dynamic-update-slice.7, f32[4]{0:T(128)S(1)} %dynamic-update-slice.15, f32[4]{0:T(128)S(1)} %dynamic-update-slice.11), channel_id=1, replica_groups=mesh['radar_0'=4,'radar_1'=2,'tile_0'=4,'tile_1'=4] {'tile_1'}, use_global_device_ids=true, to_apply=%add.24 | all-reduce | flops 12 | bytes 96
  334.8 3.6 %collective-permute-start.18 = (f32[3,16,32,1]{2,1,3,0:T(8,128)S(1)}, f32[3,16,32,1]{2,1,3,0:T(8,128)}, u32[]{:S(2)}, u32[]{:S(2)}) collective-permute-start(f32[3,16,32,1]{2,1,3,0:T(8,128)S(1)} %copy.54), channel_id=1, source_target_pairs={{16,0},{32,16},{48,32},{64,48},{80,64},{96,80},{112,96},{17,1},{33... | collective-permute-start | bytes 18440 | tf_op jit(solution)/shard_map/ppermute | solution.py:26
  338.5 4.4 %collective-permute-start.16 = (f32[3,1,32,256]{3,2,1,0:T(8,128)S(1)}, f32[3,1,32,256]{3,2,1,0:T(8,128)S(1)}, u32[]{:S(2)}, u32[]{:S(2)}) collective-permute-start(f32[3,1,32,256]{3,2,1,0:T(8,128)S(1)} %get-tuple-element.37), channel_id=1, source_target_pairs={{0,1},{1,2},{2,3},{3,4},{4,5},{5,6},{6,7},{7,8},{8,9},{9,10},{10,1... | collective-permute-start | bytes 294920 | tf_op jit(solution)/shard_map/ppermute | solution.py:25
  342.9 2.2 collective-permute-start.19
  347.1 4.4 %collective-permute-done.19 = f32[3,1,32,256]{3,2,1,0:T(8,128)S(1)} collective-permute-done((f32[3,1,32,256]{3,2,1,0:T(8,128)S(1)}, f32[3,1,32,256]{3,2,1,0:T(8,128)S(1)}, u32[]{:S(2)}, u32[]{:S(2)}) %collective-permute-start.19) | collective-permute-done | bytes 98336 | tf_op jit(solution)/shard_map/ppermute | solution.py:26
  (177 shorter events, 85.5 us)
Async XLA Ops:
  0.6 8.0 %copy-start = (f32[3,16,32,256]{3,2,1,0:T(8,128)S(1)}, f32[3,16,32,256]{3,2,1,0:T(8,128)}, u32[]{:S(2)}) copy-start(f32[3,16,32,256]{3,2,1,0:T(8,128)} %param.6) | copy-start | bytes 4718596
  0.6 13.9 %copy-start.11 = (s32[1,128]{1,0:T(1,128)S(1)}, s32[1,128]{1,0:T(1,128)}, u32[]{:S(2)}) copy-start(s32[1,128]{1,0:T(1,128)} %param.11) | copy-start | bytes 1540
  0.7 14.0 %copy-start.12 = (s32[256]{0:T(256)S(1)}, s32[256]{0:T(256)}, u32[]{:S(2)}) copy-start(s32[256]{0:T(256)} %param.10) | copy-start | bytes 3076
  3.1 40.0 %collective-permute-start.1 = (f32[2,16,32,1]{3,2,1,0:T(8,128)}, f32[2,16,32,1]{3,2,1,0:T(8,128)}, u32[]{:S(2)}, u32[]{:S(2)}) collective-permute-start(f32[2,16,32,1]{3,2,1,0:T(8,128)} %get-tuple-element.43), channel_id=1, source_target_pairs={{0,16},{16,32},{32,48},{48,64},{64,80},{80,96},{96,112},{1,17},{17... | collective-permute-start | bytes 12296 | tf_op jit(solution)/shard_map/ppermute | solution.py:25
  5.0 38.0 %collective-permute-start.2 = (f32[2,16,32,1]{3,2,1,0:T(8,128)}, f32[2,16,32,1]{3,2,1,0:T(8,128)}, u32[]{:S(2)}, u32[]{:S(2)}) collective-permute-start(f32[2,16,32,1]{3,2,1,0:T(8,128)} %get-tuple-element.44), channel_id=1, source_target_pairs={{16,0},{32,16},{48,32},{64,48},{80,64},{96,80},{112,96},{17,1},{33... | collective-permute-start | bytes 12296 | tf_op jit(solution)/shard_map/ppermute | solution.py:26
  8.7 34.4 %collective-permute-start = (f32[2,1,32,256]{3,2,1,0:T(8,128)S(1)}, f32[2,1,32,256]{3,2,1,0:T(8,128)S(1)}, u32[]{:S(2)}, u32[]{:S(2)}) collective-permute-start(f32[2,1,32,256]{3,2,1,0:T(8,128)S(1)} %get-tuple-element.45), channel_id=1, source_target_pairs={{0,1},{1,2},{2,3},{3,4},{4,5},{5,6},{6,7},{7,8},{8,9},{9,10},{10,1... | collective-permute-start | bytes 196616 | tf_op jit(solution)/shard_map/ppermute | solution.py:25
  10.8 32.3 %collective-permute-start.3 = (f32[2,1,32,256]{3,2,1,0:T(8,128)S(1)}, f32[2,1,32,256]{3,2,1,0:T(8,128)S(1)}, u32[]{:S(2)}, u32[]{:S(2)}) collective-permute-start(f32[2,1,32,256]{3,2,1,0:T(8,128)S(1)} %get-tuple-element.46), channel_id=1, source_target_pairs={{1,0},{2,1},{3,2},{4,3},{5,4},{6,5},{7,6},{8,7},{9,8},{10,9},{11,1... | collective-permute-start | bytes 196616 | tf_op jit(solution)/shard_map/ppermute | solution.py:26
  15.6 16.4 %all-to-all-start = ((s32[128,2,2]{2,1,0:T(2,128)}), s32[128,2,2]{2,1,0:T(2,128)S(1)}, u32[]{:S(2)}, u32[]{:S(2)}) async-start(s32[128,2,2]{2,1,0:T(2,128)} %copy.39), calls=%async_computation | async-start | bytes 262144 | tf_op jit(solution)/shard_map/all_to_all | solution.py:117
  25.8 17.3 %slice-start = ((f32[3,16,32,256]{3,2,1,0:T(8,128)}), f32[2,16,32,256]{3,2,1,0:T(8,128)S(1)}, s32[]{:S(2)}) async-start(f32[3,16,32,256]{3,2,1,0:T(8,128)} %param.6), calls=%async_computation.5 | async-start | bytes 2097152 | tf_op jit(solution)/shard_map/slice | solution.py:93
  35.4 18.8 %all-to-all-start.1 = ((bf16[128,3,1,1,2,128]{5,4,3,2,1,0:T(2,128)(2,1)}), bf16[128,3,1,1,2,128]{5,4,3,2,1,0:T(2,128)(2,1)S(1)}, u32[]{:S(2)}, u32[]{:S(2)}) async-start(bf16[128,3,1,1,2,128]{5,4,3,2,1,0:T(2,128)(2,1)} %bitcast.7), calls=%async_computation.1 | async-start | bytes 393216 | tf_op jit(solution)/shard_map/all_to_all | solution.py:54
  45.1 9.2 %copy-start.4 = (bf16[256,3,128]{2,0,1:T(8,128)(2,1)S(1)}, bf16[256,3,128]{2,0,1:T(8,128)(2,1)}, u32[]{:S(2)}) copy-start(bf16[256,3,128]{2,0,1:T(8,128)(2,1)} %param.8) | copy-start | bytes 589828
  46.2 42.6 %collective-permute-start.6 = (f32[1,32,256]{2,1,0:T(8,128)S(1)}, f32[1,32,256]{2,1,0:T(8,128)S(1)}, u32[]{:S(2)}, u32[]{:S(2)}) collective-permute-start(f32[1,32,256]{2,1,0:T(8,128)S(1)} %get-tuple-element.57), channel_id=1, source_target_pairs={{1,0},{2,1},{3,2},{4,3},{5,4},{6,5},{7,6},{8,7},{9,8},{10,9},{11,1... | collective-permute-start | bytes 98312 | tf_op jit(solution)/shard_map/ppermute | solution.py:26
  48.7 40.1 %collective-permute-start.7 = (f32[1,32,256]{2,1,0:T(8,128)S(1)}, f32[1,32,256]{2,1,0:T(8,128)S(1)}, u32[]{:S(2)}, u32[]{:S(2)}) collective-permute-start(f32[1,32,256]{2,1,0:T(8,128)S(1)} %get-tuple-element.58), channel_id=1, source_target_pairs={{0,1},{1,2},{2,3},{3,4},{4,5},{5,6},{6,7},{7,8},{8,9},{9,10},{10,1... | collective-permute-start | bytes 98312 | tf_op jit(solution)/shard_map/ppermute | solution.py:25
  54.3 7.9 %copy-start.8 = (bf16[256,128]{1,0:T(8,128)(2,1)S(1)}, bf16[256,128]{1,0:T(8,128)(2,1)}, u32[]{:S(2)}) copy-start(bf16[256,128]{1,0:T(8,128)(2,1)} %param.9) | copy-start | bytes 196612
  68.5 16.6 %copy-start.16 = (u32[128]{0:T(128)S(1)}, u32[128]{0:T(128)}, u32[]{:S(2)}) copy-start(u32[128]{0:T(128)} %constant.67) | copy-start | bytes 1540
  69.4 21.0 %all-to-all-start.2 = ((f32[128,3,1,1,2,128]{5,4,3,2,1,0:T(2,128)}), f32[128,3,1,1,2,128]{5,4,3,2,1,0:T(2,128)S(1)}, u32[]{:S(2)}, u32[]{:S(2)}) async-start(f32[128,3,1,1,2,128]{5,4,3,2,1,0:T(2,128)} %bitcast.18), calls=%async_computation.2 | async-start | bytes 786432 | tf_op jit(solution)/shard_map/all_to_all | solution.py:54
  79.3 7.8 %collective-permute-start.4 = (f32[16,32,1]{2,1,0:T(8,128)S(1)}, f32[16,32,1]{2,1,0:T(8,128)S(1)}, u32[]{:S(2)}, u32[]{:S(2)}) collective-permute-start(f32[16,32,1]{2,1,0:T(8,128)S(1)} %get-tuple-element.60), channel_id=1, source_target_pairs={{0,16},{16,32},{32,48},{48,64},{64,80},{80,96},{96,112},{1,17},{17... | collective-permute-start | bytes 6152 | tf_op jit(solution)/shard_map/ppermute | solution.py:25
  81.4 7.4 %collective-permute-start.5 = (f32[16,32,1]{2,1,0:T(8,128)S(1)}, f32[16,32,1]{2,1,0:T(8,128)S(1)}, u32[]{:S(2)}, u32[]{:S(2)}) collective-permute-start(f32[16,32,1]{2,1,0:T(8,128)S(1)} %get-tuple-element.59), channel_id=1, source_target_pairs={{16,0},{32,16},{48,32},{64,48},{80,64},{96,80},{112,96},{17,1},{33... | collective-permute-start | bytes 6152 | tf_op jit(solution)/shard_map/ppermute | solution.py:26
  100.5 1.9 copy-start.1
  102.3 3.0 copy-start.3
  102.4 4.3 %copy-start.15 = (u32[128]{0:T(128)S(1)}, u32[128]{0:T(128)}, u32[]{:S(2)}) copy-start(u32[128]{0:T(128)} %constant.72) | copy-start | bytes 1540
  102.4 15.5 %copy-start.14 = (u32[128]{0:T(128)S(1)}, u32[128]{0:T(128)}, u32[]{:S(2)}) copy-start(u32[128]{0:T(128)} %constant.77) | copy-start | bytes 1540
  102.4 20.6 %copy-start.13 = (u32[128]{0:T(128)S(1)}, u32[128]{0:T(128)}, u32[]{:S(2)}) copy-start(u32[128]{0:T(128)} %constant.82) | copy-start | bytes 1540
  150.1 30.9 %collective-permute-start.10 = (f32[2,16,32,1]{3,2,1,0:T(8,128)}, f32[2,16,32,1]{3,2,1,0:T(8,128)}, u32[]{:S(2)}, u32[]{:S(2)}) collective-permute-start(f32[2,16,32,1]{3,2,1,0:T(8,128)} %get-tuple-element.40), channel_id=1, source_target_pairs={{16,0},{32,16},{48,32},{64,48},{80,64},{96,80},{112,96},{17,1},{33... | collective-permute-start | bytes 12296 | tf_op jit(solution)/shard_map/ppermute | solution.py:26
  152.0 29.0 %collective-permute-start.9 = (f32[2,16,32,1]{3,2,1,0:T(8,128)}, f32[2,16,32,1]{3,2,1,0:T(8,128)}, u32[]{:S(2)}, u32[]{:S(2)}) collective-permute-start(f32[2,16,32,1]{3,2,1,0:T(8,128)} %get-tuple-element.39), channel_id=1, source_target_pairs={{0,16},{16,32},{32,48},{48,64},{64,80},{80,96},{96,112},{1,17},{17... | collective-permute-start | bytes 12296 | tf_op jit(solution)/shard_map/ppermute | solution.py:25
  154.4 26.6 %collective-permute-start.11 = (f32[2,1,32,256]{3,2,1,0:T(8,128)}, f32[2,1,32,256]{3,2,1,0:T(8,128)}, u32[]{:S(2)}, u32[]{:S(2)}) collective-permute-start(f32[2,1,32,256]{3,2,1,0:T(8,128)} %get-tuple-element.42), channel_id=1, source_target_pairs={{1,0},{2,1},{3,2},{4,3},{5,4},{6,5},{7,6},{8,7},{9,8},{10,9},{11,1... | collective-permute-start | bytes 196616 | tf_op jit(solution)/shard_map/ppermute | solution.py:26
  158.0 23.0 %collective-permute-start.8 = (f32[2,1,32,256]{3,2,1,0:T(8,128)}, f32[2,1,32,256]{3,2,1,0:T(8,128)}, u32[]{:S(2)}, u32[]{:S(2)}) collective-permute-start(f32[2,1,32,256]{3,2,1,0:T(8,128)} %get-tuple-element.41), channel_id=1, source_target_pairs={{0,1},{1,2},{2,3},{3,4},{4,5},{5,6},{6,7},{7,8},{8,9},{9,10},{10,1... | collective-permute-start | bytes 196616 | tf_op jit(solution)/shard_map/ppermute | solution.py:25
  164.3 1.5 copy-start.6
  172.1 22.9 %all-to-all-start.3 = ((bf16[128,3,1,1,2,128]{5,4,3,2,1,0:T(2,128)(2,1)}), bf16[128,3,1,1,2,128]{5,4,3,2,1,0:T(2,128)(2,1)S(1)}, u32[]{:S(2)}, u32[]{:S(2)}) async-start(bf16[128,3,1,1,2,128]{5,4,3,2,1,0:T(2,128)(2,1)} %bitcast.177), calls=%async_computation.3 | async-start | bytes 393216 | tf_op jit(solution)/shard_map/all_to_all | solution.py:54
  183.3 1.0 copy-start.7
  185.4 0.8 copy-start.5
  186.8 44.9 %collective-permute-start.14 = (f32[1,32,256]{2,1,0:T(8,128)}, f32[1,32,256]{2,1,0:T(8,128)}, u32[]{:S(2)}, u32[]{:S(2)}) collective-permute-start(f32[1,32,256]{2,1,0:T(8,128)} %get-tuple-element.52), channel_id=1, source_target_pairs={{1,0},{2,1},{3,2},{4,3},{5,4},{6,5},{7,6},{8,7},{9,8},{10,9},{11,1... | collective-permute-start | bytes 98312 | tf_op jit(solution)/shard_map/ppermute | solution.py:26
  189.3 42.4 %collective-permute-start.15 = (f32[1,32,256]{2,1,0:T(8,128)}, f32[1,32,256]{2,1,0:T(8,128)}, u32[]{:S(2)}, u32[]{:S(2)}) collective-permute-start(f32[1,32,256]{2,1,0:T(8,128)} %get-tuple-element.53), channel_id=1, source_target_pairs={{0,1},{1,2},{2,3},{3,4},{4,5},{5,6},{6,7},{7,8},{8,9},{9,10},{10,1... | collective-permute-start | bytes 98312 | tf_op jit(solution)/shard_map/ppermute | solution.py:25
  195.1 7.9 %copy-start.9 = (bf16[256,128]{1,0:T(8,128)(2,1)S(1)}, bf16[256,128]{1,0:T(8,128)(2,1)}, u32[]{:S(2)}) copy-start(bf16[256,128]{1,0:T(8,128)(2,1)} %param.9) | copy-start | bytes 196612
  210.4 27.1 %all-to-all-start.4 = ((f32[128,3,1,1,2,128]{5,4,3,2,1,0:T(2,128)}), f32[128,3,1,1,2,128]{5,4,3,2,1,0:T(2,128)S(1)}, u32[]{:S(2)}, u32[]{:S(2)}) async-start(f32[128,3,1,1,2,128]{5,4,3,2,1,0:T(2,128)} %bitcast.169), calls=%async_computation.4 | async-start | bytes 786432 | tf_op jit(solution)/shard_map/all_to_all | solution.py:54
  222.0 9.4 %collective-permute-start.12 = (f32[16,32,1]{2,1,0:T(8,128)}, f32[16,32,1]{2,1,0:T(8,128)}, u32[]{:S(2)}, u32[]{:S(2)}) collective-permute-start(f32[16,32,1]{2,1,0:T(8,128)} %get-tuple-element.55), channel_id=1, source_target_pairs={{0,16},{16,32},{32,48},{48,64},{64,80},{80,96},{96,112},{1,17},{17... | collective-permute-start | bytes 6152 | tf_op jit(solution)/shard_map/ppermute | solution.py:25
  224.1 7.7 %collective-permute-start.13 = (f32[16,32,1]{2,1,0:T(8,128)}, f32[16,32,1]{2,1,0:T(8,128)}, u32[]{:S(2)}, u32[]{:S(2)}) collective-permute-start(f32[16,32,1]{2,1,0:T(8,128)} %get-tuple-element.54), channel_id=1, source_target_pairs={{16,0},{32,16},{48,32},{64,48},{80,64},{96,80},{112,96},{17,1},{33... | collective-permute-start | bytes 6152 | tf_op jit(solution)/shard_map/ppermute | solution.py:26
  328.7 22.8 %copy-start.2 = (f32[3,16,32,256]{3,2,1,0:T(8,128)}, f32[3,16,32,256]{3,2,1,0:T(8,128)S(1)}, u32[]{:S(2)}) copy-start(f32[3,16,32,256]{3,2,1,0:T(8,128)S(1)} %divide_subtract_fusion) | copy-start | bytes 4718596
  332.6 13.1 %collective-permute-start.17 = (f32[3,16,32,1]{2,1,3,0:T(8,128)}, f32[3,16,32,1]{2,1,3,0:T(8,128)S(1)}, u32[]{:S(2)}, u32[]{:S(2)}) collective-permute-start(f32[3,16,32,1]{2,1,3,0:T(8,128)} %copy.53), channel_id=1, source_target_pairs={{0,16},{16,32},{32,48},{48,64},{64,80},{80,96},{96,112},{1,17},{17... | collective-permute-start | bytes 18440 | tf_op jit(solution)/shard_map/ppermute | solution.py:25
  334.8 11.2 %collective-permute-start.18 = (f32[3,16,32,1]{2,1,3,0:T(8,128)S(1)}, f32[3,16,32,1]{2,1,3,0:T(8,128)}, u32[]{:S(2)}, u32[]{:S(2)}) collective-permute-start(f32[3,16,32,1]{2,1,3,0:T(8,128)S(1)} %copy.54), channel_id=1, source_target_pairs={{16,0},{32,16},{48,32},{64,48},{80,64},{96,80},{112,96},{17,1},{33... | collective-permute-start | bytes 18440 | tf_op jit(solution)/shard_map/ppermute | solution.py:26
  338.5 8.7 %collective-permute-start.16 = (f32[3,1,32,256]{3,2,1,0:T(8,128)S(1)}, f32[3,1,32,256]{3,2,1,0:T(8,128)S(1)}, u32[]{:S(2)}, u32[]{:S(2)}) collective-permute-start(f32[3,1,32,256]{3,2,1,0:T(8,128)S(1)} %get-tuple-element.37), channel_id=1, source_target_pairs={{0,1},{1,2},{2,3},{3,4},{4,5},{5,6},{6,7},{7,8},{8,9},{9,10},{10,1... | collective-permute-start | bytes 294920 | tf_op jit(solution)/shard_map/ppermute | solution.py:25
  342.9 8.6 %collective-permute-start.19 = (f32[3,1,32,256]{3,2,1,0:T(8,128)S(1)}, f32[3,1,32,256]{3,2,1,0:T(8,128)S(1)}, u32[]{:S(2)}, u32[]{:S(2)}) collective-permute-start(f32[3,1,32,256]{3,2,1,0:T(8,128)S(1)} %get-tuple-element.38), channel_id=1, source_target_pairs={{1,0},{2,1},{3,2},{4,3},{5,4},{6,5},{7,6},{8,7},{9,8},{10,9},{11,1... | collective-permute-start | bytes 294920 | tf_op jit(solution)/shard_map/ppermute | solution.py:26
  355.0 1.7 copy-start.10
